TPU v7x, 32 devices: a whole 2x2x4 slice. The times are simulated.
32 devices in a mesh: grp: 4 (over z), sep: 8 (over y, x, core).
Axes of the slice: x: 2, y: 2, z: 4, core: 2. Of those that a mesh axis runs over, the one named last changes fastest.
Arguments:
- tiles: bfloat16 [4, 256, 64, 128], P('grp', 'sep'), may hold values from 0.0099487305 to 0.29882812
- tile_front: int32 [4, 256, 1], P('grp', 'sep'), may hold values from 0 to 7; in each aligned block of 32 rows (0 to 31, 32 to 63, ..., all dimensions but the last counted through in order) at most 8 rows name the same one
- tile_pos: int32 [4, 256], P('grp', 'sep'), may hold values from 0 to 29
- front_slot: int32 [4, 8], P('grp'), may hold values from 0 to 7, as said below
- front_parent: int32 [4, 8], P('grp'), may hold values from 0 to 7, as said below
- pivot: float32 [4, 8, 640], P('grp'), may hold values from 4 to 40
Outputs:
- factor: float32 [4, 8, 640, 512], P('grp', 'sep')
- sep_schur: float32 [8, 128, 128], P('sep')
Inputs may be any that keep to these rules, and one draw needn't show every extreme that they name: `tile_front`: at most 8 of the tiles held by one device belong to one front. `front_slot`: each group's row is a permutation of 0 to 7. (front_parent[g, f] - front_slot[g, f]) modulo 8 is one of 0, 1, 7 and 4; in every group each of these four occurs.
All inputs are finite; a program needn't handle non-finite values.
Results may differ from a plain program's by a relative error of at most 0.0003.
Values may be sent and summed in bfloat16 or wider, within the bound.
A program may use at most 64 MiB of HBM per device.

v0:
```python
import jax
import jax.numpy as jnp
import numpy as np
from jax import lax
from jax.sharding import PartitionSpec as P

POS = 30


def passed_along(shard, axis, by):
    devices = lax.axis_size(axis)
    return lax.ppermute(shard, axis, [(i, (i + by) % devices) for i in range(devices)])


def tile_arrangement(rows, column_indices):
    row_count = 5 * column_indices // rows
    position = np.zeros((row_count, 5), np.int32)
    present = np.zeros((row_count, 5), np.float32)
    number = 0
    for row_block in range(row_count):
        for col_block in range(row_block * rows // column_indices + 1):
            position[row_block, col_block] = number
            present[row_block, col_block] = 1.0
            number += 1
    return (position, present)


def front_factor(summed, pivots, rows, column_indices):
    position, present = tile_arrangement(rows, column_indices)
    order = 5 * column_indices
    elimination_count = 4 * column_indices
    blocks = summed[position] * jnp.asarray(present, jnp.float32)[:, :, None, None]
    full = blocks.transpose(0, 2, 1, 3).reshape(order, order)
    mixed = 0.5 * (full + full.T) * (1.0 - jnp.eye(order, dtype=jnp.float32))
    front_matrix = jnp.diag(pivots + jnp.sum(mixed, 1)) - mixed
    lower_triangle = jnp.linalg.cholesky(front_matrix[:elimination_count, :elimination_count])
    under_diagonal = jax.scipy.linalg.solve_triangular(
        lower_triangle, front_matrix[elimination_count:, :elimination_count].T, lower=True
    ).T
    schur = jnp.dot(under_diagonal, under_diagonal.T, precision=lax.Precision.HIGHEST)
    return (jnp.concatenate([lower_triangle, under_diagonal], 0), schur)


def body(tiles, tile_front, tile_pos, front_slot, front_parent, pivot):
    width = lax.axis_size("sep")
    myself = lax.axis_index("sep")
    held = tiles.shape[1]
    rows = tiles.shape[2]
    column_indices = tiles.shape[3]
    fronts = front_slot.shape[1]
    room = max(2, -(-2 * held // width))
    slots = front_slot[0]
    parents = front_parent[0]
    front_ids = jnp.arange(fronts, dtype=jnp.int32)
    owner_of = jnp.sum(jnp.where(tile_front[0] == front_ids[None, :], slots[None, :], 0), 1)
    target = (owner_of[:, None] == jnp.arange(width, dtype=jnp.int32)[None, :]).astype(jnp.int32)
    rank = jnp.sum(target * (jnp.cumsum(target, 0) - 1), 1)
    place = owner_of * room + rank
    outgoing = jnp.zeros((width * room, rows, column_indices), jnp.bfloat16).at[place].set(tiles[0])
    labels = jnp.full((width * room,), -1, jnp.int32).at[place].set(tile_pos[0])
    arrived, received_position = (
        lax.all_to_all(
            outgoing.reshape(width, room, rows, column_indices),
            "sep",
            split_axis=0,
            concat_axis=0,
            tiled=True,
        ),
        lax.all_to_all(labels.reshape(width, room), "sep", split_axis=0, concat_axis=0, tiled=True),
    )
    arrived = arrived.reshape(width * room, rows, column_indices)
    received_position = received_position.reshape(width * room)
    selector = (received_position[None, :] == jnp.arange(POS, dtype=jnp.int32)[:, None]).astype(
        jnp.bfloat16
    )
    summed = jnp.einsum("ps,sij->pij", selector, arrived, preferred_element_type=jnp.float32)
    mine = slots == myself
    pivots = jnp.sum(jnp.where(mine[:, None], pivot[0], 0.0), 0)
    parent = jnp.sum(jnp.where(mine, parents, 0))
    factor, schur = front_factor(summed, pivots, rows, column_indices)
    distance = (parent - myself) % width
    local_sum = jnp.where(distance == 0, schur, 0.0)[None]
    for offset in (1, -1, width // 2):
        piece = jnp.where(distance == offset % width, schur, 0.0)[None]
        local_sum = local_sum + passed_along(piece, "sep", offset)
    total = lax.psum(local_sum, "grp")
    return (factor[None, None], total)


def solution(mesh):
    placed = (
        P("grp", "sep", None, None),
        P("grp", "sep", None),
        P("grp", "sep"),
        P("grp", None),
        P("grp", None),
        P("grp", None, None),
    )
    return jax.shard_map(
        body,
        mesh=mesh,
        in_specs=placed,
        out_specs=(P("grp", "sep", None, None), P("sep", None, None)),
        check_vma=False,
    )
```

profile of v0, /device:TPU:0, one launch (start us, length us, event | category | flops | bytes accessed | tf_op | source)
XLA Modules:
  0.0 244.2 jit_solution(3018031008141978505)
XLA Ops:
  9.8 5.2 %all-to-all-start = ((s32[8,1,8]{2,1,0:T(1,128)}), s32[8,1,8]{2,1,0:T(1,128)S(1)}, u32[]{:S(2)}, u32[]{:S(2)}) async-start(s32[8,1,8]{2,1,0:T(1,128)} %bitcast.6), calls=%async_computation | async-start | bytes 8192 | tf_op jit(solution)/shard_map/all_to_all | solution.py:69
  15.3 3.4 %scatter_fusion = bf16[64,64,128]{2,1,0:T(8,128)(2,1)S(1)} fusion(bf16[64,64,128]{2,1,0:T(8,128)(2,1)S(1)} %broadcast_in_dim.90, s32[32]{0:T(128)S(1)} %fusion.44, bf16[32,64,128]{2,1,0:T(8,128)(2,1)} %bitcast.120), kind=kCustom, calls=%fused_computation.2 | custom fusion | bytes 1572992 | tf_op jit(solution)/shard_map/scatter | solution.py:59
  18.7 1.7 copy.28
  20.4 4.2 %all-to-all-start.1 = ((bf16[8,8,64,128]{3,1,2,0:T(8,128)(2,1)}), bf16[8,8,64,128]{3,1,2,0:T(8,128)(2,1)S(1)}, u32[]{:S(2)}, u32[]{:S(2)}) async-start(bf16[8,8,64,128]{3,1,2,0:T(8,128)(2,1)} %copy.28), calls=%async_computation.1 | async-start | bytes 2097152 | tf_op jit(solution)/shard_map/all_to_all | solution.py:62
  27.4 12.6 %all-to-all-done.1 = bf16[8,8,64,128]{3,1,2,0:T(8,128)(2,1)S(1)} async-done(((bf16[8,8,64,128]{3,1,2,0:T(8,128)(2,1)}), bf16[8,8,64,128]{3,1,2,0:T(8,128)(2,1)S(1)}, u32[]{:S(2)}, u32[]{:S(2)}) %all-to-all-start.1) | async-done | bytes 1048608 | tf_op jit(solution)/shard_map/all_to_all | solution.py:62
  42.7 1.6 copy.49
  44.3 2.7 %copy.32 = f32[640,640]{0,1:T(8,128)} copy(f32[640,640]{1,0:T(8,128)} %bitcast.118) | data formatting | bytes 3276800 | tf_op jit(solution)/shard_map/reshape | solution.py:33
  47.0 2.0 fusion.7
  49.5 1.3 slice.135
  51.1 1.7 copy.33
  54.0 11.7 %cholesky.104 = f32[128,128]{1,0:T(8,128)S(1)} custom-call(f32[128,128]{1,0:T(8,128)S(1)} %cholesky.266), custom_call_target="Cholesky" | custom-call | tf_op jit(solution)/shard_map/jit(cholesky)/cholesky | solution.py:36
  65.7 9.8 %custom-call.31 = f32[1,128,128]{1,2,0:T(8,128)S(1)} custom-call(f32[1,128,128]{2,1,0:T(8,128)S(1)} %get-tuple-element.36), custom_call_target="InvertDiagBlocksLowerTriangular" | custom-call | tf_op jit(solution)/shard_map/jit(cholesky)/cholesky | solution.py:36
  75.7 1.2 constant_dynamic-update-slice_fusion.3
  76.9 1.3 convolution_subtract_fusion
  78.2 11.7 %cholesky.217 = f32[128,128]{1,0:T(8,128)S(1)} custom-call(f32[128,128]{1,0:T(8,128)S(1)} %cholesky.270), custom_call_target="Cholesky" | custom-call | tf_op jit(solution)/shard_map/jit(cholesky)/cholesky | solution.py:36
  89.9 9.9 %custom-call.32 = f32[1,128,128]{1,2,0:T(8,128)S(1)} custom-call(f32[1,128,128]{2,1,0:T(8,128)S(1)} %get-tuple-element.33), custom_call_target="InvertDiagBlocksLowerTriangular" | custom-call | tf_op jit(solution)/shard_map/jit(cholesky)/cholesky | solution.py:36
  100.1 1.3 convolution_subtract_fusion.1
  101.4 11.7 %cholesky.238 = f32[128,128]{1,0:T(8,128)S(1)} custom-call(f32[128,128]{1,0:T(8,128)S(1)} %cholesky.275), custom_call_target="Cholesky" | custom-call | tf_op jit(solution)/shard_map/jit(cholesky)/cholesky | solution.py:36
  113.9 9.8 %custom-call.33 = f32[1,128,128]{1,2,0:T(8,128)S(1)} custom-call(f32[1,128,128]{2,1,0:T(8,128)S(1)} %get-tuple-element.30), custom_call_target="InvertDiagBlocksLowerTriangular" | custom-call | tf_op jit(solution)/shard_map/jit(cholesky)/cholesky | solution.py:36
  123.9 1.2 convolution_subtract_fusion.5
  125.1 11.9 %cholesky.255 = f32[128,128]{1,0:T(8,128)S(1)} custom-call(f32[128,128]{1,0:T(8,128)S(1)} %convolution_subtract_fusion.5), custom_call_target="Cholesky" | custom-call | tf_op jit(solution)/shard_map/jit(cholesky)/cholesky | solution.py:36
  141.2 10.4 %while.1 = (s32[]{:T(128)}, f32[512,512]{1,0:T(8,128)S(1)}, s32[4,2]{0,1:T(2,128)S(1)}, f32[4,128,128]{2,1,0:T(8,128)}, s32[]{:T(128)}) while((s32[]{:T(128)}, f32[512,512]{1,0:T(8,128)S(1)}, s32[4,2]{0,1:T(2,128)S(1)}, f32[4,128,128]{2,1,0:T(8,128)}, s32[]{:T(128)}) %tuple.35), condition=%wide.while_cond, body=%wide.while_body.sunk | while | flops 2 | bytes 132705 | solution.py:37
  141.8 2.0 bitcast_dynamic-update-slice_fusion.2
  144.4 2.0 bitcast_dynamic-update-slice_fusion.2
  147.0 2.0 bitcast_dynamic-update-slice_fusion.2
  149.6 2.0 bitcast_dynamic-update-slice_fusion.2
  151.6 40.1 %custom-call.34 = f32[4,128,128]{1,2,0:T(8,128)S(1)} custom-call(f32[4,128,128]{2,1,0:T(8,128)} %get-tuple-element.9), custom_call_target="InvertDiagBlocksLowerTriangular" | custom-call | tf_op jit(solution)/shard_map/jit(_solve_triangular)/triangular_solve | solution.py:37
  194.5 2.6 %collective-permute-start.1 = (f32[1,128,128]{2,1,0:T(8,128)S(1)}, f32[1,128,128]{2,1,0:T(8,128)S(1)}, u32[]{:S(2)}, u32[]{:S(2)}) collective-permute-start(f32[1,128,128]{2,1,0:T(8,128)S(1)} %get-tuple-element.26), channel_id=1, source_target_pairs={{0,7},{1,0},{2,1},{3,2},{4,3},{5,4},{6,5},{7,6},{8,15},{9,8},{10,9... | collective-permute-start | bytes 196616 | tf_op jit(solution)/shard_map/ppermute | solution.py:12
  197.7 2.0 collective-permute-done
  199.7 1.6 collective-permute-done.2
  203.2 32.7 %all-reduce.3.cloned.1.call-done = f32[1,128,128]{2,1,0:T(8,128)} async-done(((f32[1,128,128]{2,1,0:T(8,128)}), f32[1,128,128]{2,1,0:T(8,128)}) %all-reduce.3.cloned.1.call-update) | async-done | bytes 65552 | tf_op jit(solution)/shard_map/psum | solution.py:86
  235.9 1.5 copy.66
  (87 shorter events, 20.0 us)
Async XLA Ops:
  9.8 10.6 %all-to-all-start = ((s32[8,1,8]{2,1,0:T(1,128)}), s32[8,1,8]{2,1,0:T(1,128)S(1)}, u32[]{:S(2)}, u32[]{:S(2)}) async-start(s32[8,1,8]{2,1,0:T(1,128)} %bitcast.6), calls=%async_computation | async-start | bytes 8192 | tf_op jit(solution)/shard_map/all_to_all | solution.py:69
  18.7 6.0 %copy-start.6 = (s32[1,8]{1,0:T(1,128)S(1)}, s32[1,8]{1,0:T(1,128)}, u32[]{:S(2)}) copy-start(s32[1,8]{1,0:T(1,128)} %param.13) | copy-start | bytes 100
  18.7 6.0 %copy-start.7 = (s32[1,8]{1,0:T(1,128)S(1)}, s32[1,8]{1,0:T(1,128)}, u32[]{:S(2)}) copy-start(s32[1,8]{1,0:T(1,128)} %param.12) | copy-start | bytes 100
  18.7 7.3 %copy-start.8 = (s32[50]{0:T(128)S(1)}, s32[50]{0:T(128)}, u32[]{:S(2)}) copy-start(s32[50]{0:T(128)} %constant.222) | copy-start | bytes 604
  18.7 7.3 %copy-start.4 = (f32[1,8,640]{2,1,0:T(8,128)S(1)}, f32[1,8,640]{2,1,0:T(8,128)}, u32[]{:S(2)}) copy-start(f32[1,8,640]{2,1,0:T(8,128)} %param.14) | copy-start | bytes 61444
  20.4 19.6 %all-to-all-start.1 = ((bf16[8,8,64,128]{3,1,2,0:T(8,128)(2,1)}), bf16[8,8,64,128]{3,1,2,0:T(8,128)(2,1)S(1)}, u32[]{:S(2)}, u32[]{:S(2)}) async-start(bf16[8,8,64,128]{3,1,2,0:T(8,128)(2,1)} %copy.28), calls=%async_computation.1 | async-start | bytes 2097152 | tf_op jit(solution)/shard_map/all_to_all | solution.py:62
  24.6 211.2 %all-reduce.3.cloned.1.call-start = ((), (), s32[]{:S(2)}) async-start(), calls=%async_computation.2 | async-start | bytes 131072 | tf_op jit(solution)/shard_map/psum | solution.py:86
  40.9 0.7 copy-start.5
  47.0 2.0 copy-start
  49.5 1.5 copy-start.1
  51.1 1.7 copy-start.2
  53.0 1.0 copy-start.3
  194.4 5.3 %collective-permute-start = (f32[1,128,128]{2,1,0:T(8,128)S(1)}, f32[1,128,128]{2,1,0:T(8,128)S(1)}, u32[]{:S(2)}, u32[]{:S(2)}) collective-permute-start(f32[1,128,128]{2,1,0:T(8,128)S(1)} %get-tuple-element.24), channel_id=1, source_target_pairs={{0,1},{1,2},{2,3},{3,4},{4,5},{5,6},{6,7},{7,0},{8,9},{9,10},{10,1... | collective-permute-start | bytes 196616 | tf_op jit(solution)/shard_map/ppermute | solution.py:12
  194.5 5.3 %collective-permute-start.1 = (f32[1,128,128]{2,1,0:T(8,128)S(1)}, f32[1,128,128]{2,1,0:T(8,128)S(1)}, u32[]{:S(2)}, u32[]{:S(2)}) collective-permute-start(f32[1,128,128]{2,1,0:T(8,128)S(1)} %get-tuple-element.26), channel_id=1, source_target_pairs={{0,7},{1,0},{2,1},{3,2},{4,3},{5,4},{6,5},{7,6},{8,15},{9,8},{10,9... | collective-permute-start | bytes 196616 | tf_op jit(solution)/shard_map/ppermute | solution.py:12
  197.1 4.3 %collective-permute-start.2 = (f32[1,128,128]{2,1,0:T(8,128)S(1)}, f32[1,128,128]{2,1,0:T(8,128)S(1)}, u32[]{:S(2)}, u32[]{:S(2)}) collective-permute-start(f32[1,128,128]{2,1,0:T(8,128)S(1)} %get-tuple-element.25), channel_id=1, source_target_pairs={{0,4},{1,5},{2,6},{3,7},{4,0},{5,1},{6,2},{7,3},{8,12},{9,13},{10,... | collective-permute-start | bytes 196616 | tf_op jit(solution)/shard_map/ppermute | solution.py:12
Sparse Core Ops, SparseCore 0:
  202.1 33.6 all-reduce.2
where the time goes:
time: 245 us; the launch traced here: 244 us
  other arithmetic  126 us (51%)
  waiting for transfers between devices  49 us (20%)
  local copies, waits for them, and re-layouts  30.5 us (12%)
  between operations  17.7 us (7%)
  starting transfers between devices  12.7 us (5%)
  matrix products  8.06 us (3%)
    another operation x14, other arithmetic, front_factor(): jnp.linalg.cholesky(front_matrix[:elimination_count, :elimination_count])  78.7 us
    another operation x3, other arithmetic, front_factor(): jax.scipy.linalg.solve_triangular(lower_triangle, front_matrix[eliminatio...  40.4 us
    psum x1, waiting for transfers between devices, body(): total = lax.psum(local_sum, 'grp')  32.7 us
    all_to_all x1, waiting for transfers between devices, body(): lax.all_to_all(outgoing.reshape(width, room, rows, column_indices), 'sep'...  12.6 us
    another operation x12, local copies, waits for them, and re-layouts  10.4 us
    another operation x6, matrix products, front_factor(): jnp.linalg.cholesky(front_matrix[:elimination_count, :elimination_count])  5.47 us
    all_to_all x1, starting transfers between devices, body(): lax.all_to_all(labels.reshape(width, room), 'sep', split_axis=0, concat_a...  5.2 us
  transfers between devices with their start and end apart: 6, of which 4 were waited for; matrix products, arithmetic and copies ran while one was open for 3% of the time, Pallas kernels for 0%

commit v1 on v0

--- a/solution.py
+++ b/solution.py
@@ -83,7 +83,9 @@
     for offset in (1, -1, width // 2):
         piece = jnp.where(distance == offset % width, schur, 0.0)[None]
         local_sum = local_sum + passed_along(piece, "sep", offset)
-    total = lax.psum(local_sum, "grp")
+    total = local_sum
+    for hop in (1, 2):
+        total = total + lax.ppermute(total, "grp", [(dev, dev ^ hop) for dev in range(4)])
     return (factor[None, None], total)
 
 

time: 245 us -> 206 us (0.84)
  waiting for transfers between devices: 49 us -> 19.9 us
  between operations: 17.7 us -> 4.35 us
  starting transfers between devices: 12.7 us -> 17.4 us
    psum x1 -> x0, waiting for transfers between devices: 32.7 us -> none  [body(): total = lax.psum(local_sum, 'grp')]
    ppermute x0 -> x2, starting transfers between devices: none -> 4.8 us  [body(): lax.ppermute(total, 'grp', [(dev, dev ^ hop) for dev in range(4)])]
    ppermute x0 -> x2, waiting for transfers between devices: none -> 3.77 us  [body(): lax.ppermute(total, 'grp', [(dev, dev ^ hop) for dev in range(4)])]
  transfers between devices with their start and end apart: 6 -> 7, of which waited for: 4 -> 5; matrix products, arithmetic and copies ran while one was open for 3% -> 4% of each run, Pallas kernels for 0% -> 0%
where the time goes in v1:
time: 206 us
  other arithmetic  126 us (61%)
  local copies, waits for them, and re-layouts  29.5 us (14%)
  waiting for transfers between devices  19.9 us (10%)
  starting transfers between devices  17.4 us (8%)
  matrix products  8.07 us (4%)
  between operations  4.35 us (2%)
    another operation x14, other arithmetic, front_factor(): jnp.linalg.cholesky(front_matrix[:elimination_count, :elimination_count])  78.7 us
    another operation x3, other arithmetic, front_factor(): jax.scipy.linalg.solve_triangular(lower_triangle, front_matrix[eliminatio...  40.4 us
    all_to_all x1, waiting for transfers between devices, body(): lax.all_to_all(outgoing.reshape(width, room, rows, column_indices), 'sep'...  12.4 us
    another operation x12, local copies, waits for them, and re-layouts  10.9 us
    another operation x6, matrix products, front_factor(): jnp.linalg.cholesky(front_matrix[:elimination_count, :elimination_count])  5.47 us
    all_to_all x1, starting transfers between devices, body(): lax.all_to_all(labels.reshape(width, room), 'sep', split_axis=0, concat_a...  5.2 us
    ppermute x2, starting transfers between devices, body(): lax.ppermute(total, 'grp', [(dev, dev ^ hop) for dev in range(4)])  4.8 us
    all_to_all x1, starting transfers between devices, body(): lax.all_to_all(outgoing.reshape(width, room, rows, column_indices), 'sep'...  4.2 us
  transfers between devices with their start and end apart: 7, of which 5 were waited for; matrix products, arithmetic and copies ran while one was open for 4% of the time, Pallas kernels for 0%

profile of v1, /device:TPU:0, one launch (start us, length us, event | category | flops | bytes accessed | tf_op | source)
XLA Modules:
  0.0 205.7 jit_solution(17288341231316802575)
XLA Ops:
  3.3 5.2 %all-to-all-start = ((s32[8,1,8]{2,1,0:T(1,128)}), s32[8,1,8]{2,1,0:T(1,128)S(1)}, u32[]{:S(2)}, u32[]{:S(2)}) async-start(s32[8,1,8]{2,1,0:T(1,128)} %bitcast.6), calls=%async_computation | async-start | bytes 8192 | tf_op jit(solution)/shard_map/all_to_all | solution.py:69
  8.7 3.4 %scatter_fusion = bf16[64,64,128]{2,1,0:T(8,128)(2,1)S(1)} fusion(bf16[64,64,128]{2,1,0:T(8,128)(2,1)S(1)} %broadcast_in_dim.90, s32[32]{0:T(128)S(1)} %fusion.44, bf16[32,64,128]{2,1,0:T(8,128)(2,1)} %bitcast.120), kind=kCustom, calls=%fused_computation.2 | custom fusion | bytes 1572992 | tf_op jit(solution)/shard_map/scatter | solution.py:59
  12.2 1.7 copy.28
  13.9 4.2 %all-to-all-start.1 = ((bf16[8,8,64,128]{3,1,2,0:T(8,128)(2,1)}), bf16[8,8,64,128]{3,1,2,0:T(8,128)(2,1)S(1)}, u32[]{:S(2)}, u32[]{:S(2)}) async-start(bf16[8,8,64,128]{3,1,2,0:T(8,128)(2,1)} %copy.28), calls=%async_computation.1 | async-start | bytes 2097152 | tf_op jit(solution)/shard_map/all_to_all | solution.py:62
  21.0 12.4 %all-to-all-done.1 = bf16[8,8,64,128]{3,1,2,0:T(8,128)(2,1)S(1)} async-done(((bf16[8,8,64,128]{3,1,2,0:T(8,128)(2,1)}), bf16[8,8,64,128]{3,1,2,0:T(8,128)(2,1)S(1)}, u32[]{:S(2)}, u32[]{:S(2)}) %all-to-all-start.1) | async-done | bytes 1048608 | tf_op jit(solution)/shard_map/all_to_all | solution.py:62
  36.2 1.6 copy.49
  37.8 2.7 %copy.32 = f32[640,640]{0,1:T(8,128)} copy(f32[640,640]{1,0:T(8,128)} %bitcast.118) | data formatting | bytes 3276800 | tf_op jit(solution)/shard_map/reshape | solution.py:33
  40.5 2.0 fusion.7
  43.0 1.2 slice.135
  44.6 1.7 copy.33
  47.4 11.7 %cholesky.104 = f32[128,128]{1,0:T(8,128)S(1)} custom-call(f32[128,128]{1,0:T(8,128)S(1)} %cholesky.266), custom_call_target="Cholesky" | custom-call | tf_op jit(solution)/shard_map/jit(cholesky)/cholesky | solution.py:36
  59.2 9.8 %custom-call.31 = f32[1,128,128]{1,2,0:T(8,128)S(1)} custom-call(f32[1,128,128]{2,1,0:T(8,128)S(1)} %get-tuple-element.36), custom_call_target="InvertDiagBlocksLowerTriangular" | custom-call | tf_op jit(solution)/shard_map/jit(cholesky)/cholesky | solution.py:36
  69.1 1.2 constant_dynamic-update-slice_fusion.3
  70.4 1.3 convolution_subtract_fusion
  71.6 11.7 %cholesky.217 = f32[128,128]{1,0:T(8,128)S(1)} custom-call(f32[128,128]{1,0:T(8,128)S(1)} %cholesky.270), custom_call_target="Cholesky" | custom-call | tf_op jit(solution)/shard_map/jit(cholesky)/cholesky | solution.py:36
  83.4 9.9 %custom-call.32 = f32[1,128,128]{1,2,0:T(8,128)S(1)} custom-call(f32[1,128,128]{2,1,0:T(8,128)S(1)} %get-tuple-element.33), custom_call_target="InvertDiagBlocksLowerTriangular" | custom-call | tf_op jit(solution)/shard_map/jit(cholesky)/cholesky | solution.py:36
  93.6 1.3 convolution_subtract_fusion.1
  94.9 11.7 %cholesky.238 = f32[128,128]{1,0:T(8,128)S(1)} custom-call(f32[128,128]{1,0:T(8,128)S(1)} %cholesky.275), custom_call_target="Cholesky" | custom-call | tf_op jit(solution)/shard_map/jit(cholesky)/cholesky | solution.py:36
  107.3 9.8 %custom-call.33 = f32[1,128,128]{1,2,0:T(8,128)S(1)} custom-call(f32[1,128,128]{2,1,0:T(8,128)S(1)} %get-tuple-element.30), custom_call_target="InvertDiagBlocksLowerTriangular" | custom-call | tf_op jit(solution)/shard_map/jit(cholesky)/cholesky | solution.py:36
  118.6 11.9 %cholesky.255 = f32[128,128]{1,0:T(8,128)S(1)} custom-call(f32[128,128]{1,0:T(8,128)S(1)} %convolution_subtract_fusion.5), custom_call_target="Cholesky" | custom-call | tf_op jit(solution)/shard_map/jit(cholesky)/cholesky | solution.py:36
  134.6 10.9 %while.1 = (s32[]{:T(128)}, f32[512,512]{1,0:T(8,128)S(1)}, s32[4,2]{0,1:T(2,128)S(1)}, f32[4,128,128]{2,1,0:T(8,128)}, s32[]{:T(128)}) while((s32[]{:T(128)}, f32[512,512]{1,0:T(8,128)S(1)}, s32[4,2]{0,1:T(2,128)S(1)}, f32[4,128,128]{2,1,0:T(8,128)}, s32[]{:T(128)}) %tuple.35), condition=%wide.while_cond, body=%wide.while_body.sunk | while | flops 2 | bytes 132705 | solution.py:37
  135.3 2.0 bitcast_dynamic-update-slice_fusion.2
  138.0 2.0 bitcast_dynamic-update-slice_fusion.2
  140.8 2.1 bitcast_dynamic-update-slice_fusion.2
  143.5 2.0 bitcast_dynamic-update-slice_fusion.2
  145.5 40.1 %custom-call.34 = f32[4,128,128]{1,2,0:T(8,128)S(1)} custom-call(f32[4,128,128]{2,1,0:T(8,128)} %get-tuple-element.9), custom_call_target="InvertDiagBlocksLowerTriangular" | custom-call | tf_op jit(solution)/shard_map/jit(_solve_triangular)/triangular_solve | solution.py:37
  188.4 2.6 %collective-permute-start.1 = (f32[1,128,128]{2,1,0:T(8,128)S(1)}, f32[1,128,128]{2,1,0:T(8,128)S(1)}, u32[]{:S(2)}, u32[]{:S(2)}) collective-permute-start(f32[1,128,128]{2,1,0:T(8,128)S(1)} %get-tuple-element.26), channel_id=1, source_target_pairs={{0,7},{1,0},{2,1},{3,2},{4,3},{5,4},{6,5},{7,6},{8,15},{9,8},{10,9... | collective-permute-start | bytes 196616 | tf_op jit(solution)/shard_map/ppermute | solution.py:12
  191.6 2.1 %collective-permute-done = f32[1,128,128]{2,1,0:T(8,128)S(1)} collective-permute-done((f32[1,128,128]{2,1,0:T(8,128)S(1)}, f32[1,128,128]{2,1,0:T(8,128)S(1)}, u32[]{:S(2)}, u32[]{:S(2)}) %collective-permute-start) | collective-permute-done | bytes 65568 | tf_op jit(solution)/shard_map/ppermute | solution.py:12
  193.7 1.6 collective-permute-done.2
  195.3 1.6 collective-permute-start.3
  197.0 2.7 %collective-permute-done.3 = f32[1,128,128]{2,1,0:T(8,128)S(1)} collective-permute-done((f32[1,128,128]{2,1,0:T(8,128)S(1)}, f32[1,128,128]{2,1,0:T(8,128)S(1)}, u32[]{:S(2)}, u32[]{:S(2)}) %collective-permute-start.3) | collective-permute-done | bytes 65568 | tf_op jit(solution)/shard_map/ppermute | solution.py:88
  199.7 3.2 %collective-permute-start.4 = (f32[1,128,128]{2,1,0:T(8,128)S(1)}, f32[1,128,128]{2,1,0:T(8,128)S(1)}, u32[]{:S(2)}, u32[]{:S(2)}) collective-permute-start(f32[1,128,128]{2,1,0:T(8,128)S(1)} %add.113), channel_id=1, source_target_pairs={{0,16},{8,24},{16,0},{24,8},{1,17},{9,25},{17,1},{25,9},{2,18},{10... | collective-permute-start | bytes 196616 | tf_op jit(solution)/shard_map/ppermute | solution.py:88
  (89 shorter events, 22.8 us)
Async XLA Ops:
  3.3 10.6 %all-to-all-start = ((s32[8,1,8]{2,1,0:T(1,128)}), s32[8,1,8]{2,1,0:T(1,128)S(1)}, u32[]{:S(2)}, u32[]{:S(2)}) async-start(s32[8,1,8]{2,1,0:T(1,128)} %bitcast.6), calls=%async_computation | async-start | bytes 8192 | tf_op jit(solution)/shard_map/all_to_all | solution.py:69
  12.1 6.0 %copy-start.6 = (s32[1,8]{1,0:T(1,128)S(1)}, s32[1,8]{1,0:T(1,128)}, u32[]{:S(2)}) copy-start(s32[1,8]{1,0:T(1,128)} %param.13) | copy-start | bytes 100
  12.1 5.9 %copy-start.7 = (s32[1,8]{1,0:T(1,128)S(1)}, s32[1,8]{1,0:T(1,128)}, u32[]{:S(2)}) copy-start(s32[1,8]{1,0:T(1,128)} %param.12) | copy-start | bytes 100
  12.1 7.4 %copy-start.8 = (s32[50]{0:T(128)S(1)}, s32[50]{0:T(128)}, u32[]{:S(2)}) copy-start(s32[50]{0:T(128)} %constant.222) | copy-start | bytes 604
  12.2 7.4 %copy-start.4 = (f32[1,8,640]{2,1,0:T(8,128)S(1)}, f32[1,8,640]{2,1,0:T(8,128)}, u32[]{:S(2)}) copy-start(f32[1,8,640]{2,1,0:T(8,128)} %param.14) | copy-start | bytes 61444
  13.9 19.6 %all-to-all-start.1 = ((bf16[8,8,64,128]{3,1,2,0:T(8,128)(2,1)}), bf16[8,8,64,128]{3,1,2,0:T(8,128)(2,1)S(1)}, u32[]{:S(2)}, u32[]{:S(2)}) async-start(bf16[8,8,64,128]{3,1,2,0:T(8,128)(2,1)} %copy.28), calls=%async_computation.1 | async-start | bytes 2097152 | tf_op jit(solution)/shard_map/all_to_all | solution.py:62
  34.3 0.7 copy-start.5
  40.5 2.0 copy-start
  43.0 1.5 copy-start.1
  44.5 1.7 copy-start.2
  46.4 1.0 copy-start.3
  188.3 5.3 %collective-permute-start = (f32[1,128,128]{2,1,0:T(8,128)S(1)}, f32[1,128,128]{2,1,0:T(8,128)S(1)}, u32[]{:S(2)}, u32[]{:S(2)}) collective-permute-start(f32[1,128,128]{2,1,0:T(8,128)S(1)} %get-tuple-element.24), channel_id=1, source_target_pairs={{0,1},{1,2},{2,3},{3,4},{4,5},{5,6},{6,7},{7,0},{8,9},{9,10},{10,1... | collective-permute-start | bytes 196616 | tf_op jit(solution)/shard_map/ppermute | solution.py:12
  188.4 5.3 %collective-permute-start.1 = (f32[1,128,128]{2,1,0:T(8,128)S(1)}, f32[1,128,128]{2,1,0:T(8,128)S(1)}, u32[]{:S(2)}, u32[]{:S(2)}) collective-permute-start(f32[1,128,128]{2,1,0:T(8,128)S(1)} %get-tuple-element.26), channel_id=1, source_target_pairs={{0,7},{1,0},{2,1},{3,2},{4,3},{5,4},{6,5},{7,6},{8,15},{9,8},{10,9... | collective-permute-start | bytes 196616 | tf_op jit(solution)/shard_map/ppermute | solution.py:12
  191.0 4.3 %collective-permute-start.2 = (f32[1,128,128]{2,1,0:T(8,128)S(1)}, f32[1,128,128]{2,1,0:T(8,128)S(1)}, u32[]{:S(2)}, u32[]{:S(2)}) collective-permute-start(f32[1,128,128]{2,1,0:T(8,128)S(1)} %get-tuple-element.25), channel_id=1, source_target_pairs={{0,4},{1,5},{2,6},{3,7},{4,0},{5,1},{6,2},{7,3},{8,12},{9,13},{10,... | collective-permute-start | bytes 196616 | tf_op jit(solution)/shard_map/ppermute | solution.py:12
  195.3 4.3 %collective-permute-start.3 = (f32[1,128,128]{2,1,0:T(8,128)S(1)}, f32[1,128,128]{2,1,0:T(8,128)S(1)}, u32[]{:S(2)}, u32[]{:S(2)}) collective-permute-start(f32[1,128,128]{2,1,0:T(8,128)S(1)} %fusion.35), channel_id=1, source_target_pairs={{0,8},{8,0},{16,24},{24,16},{1,9},{9,1},{17,25},{25,17},{2,10},{10... | collective-permute-start | bytes 196616 | tf_op jit(solution)/shard_map/ppermute | solution.py:88
  199.7 5.4 %collective-permute-start.4 = (f32[1,128,128]{2,1,0:T(8,128)S(1)}, f32[1,128,128]{2,1,0:T(8,128)S(1)}, u32[]{:S(2)}, u32[]{:S(2)}) collective-permute-start(f32[1,128,128]{2,1,0:T(8,128)S(1)} %add.113), channel_id=1, source_target_pairs={{0,16},{8,24},{16,0},{24,8},{1,17},{9,25},{17,1},{25,9},{2,18},{10... | collective-permute-start | bytes 196616 | tf_op jit(solution)/shard_map/ppermute | solution.py:88
